TPU v7x, 32 devices: a whole 2x2x4 slice. The times are simulated.
32 devices in a mesh: rows: 4 (over y, x), cols: 8 (over z, core).
Axes of the slice: x: 2, y: 2, z: 4, core: 2. Of those that a mesh axis runs over, the one named last changes fastest.
Arguments:
- tokens: bfloat16 [128, 256, 256], P('rows', 'cols'), may hold values from -45 to 45
- key_bias: bfloat16 [128, 256], P('rows', 'cols'), may hold values from -3 to 250
- cotangent: bfloat16 [128, 256, 256], P('rows', 'cols'), may hold values from -6 to 6
- gain_row: float32 [256], replicated, may hold values from 0.1 to 1.9
- w_qkv_row: bfloat16 [256, 768], replicated, may hold values from -0.375 to 0.375
- w_out_row: bfloat16 [256, 256], replicated, may hold values from -0.375 to 0.375
- gain_col: float32 [256], replicated, may hold values from 0.1 to 1.9
- w_qkv_col: bfloat16 [256, 768], replicated, may hold values from -0.375 to 0.375
- w_out_col: bfloat16 [256, 256], replicated, may hold values from -0.375 to 0.375
- gain_mlp: float32 [256], replicated, may hold values from 0.1 to 1.9
- w_up: bfloat16 [256, 1024], replicated, may hold values from -0.375 to 0.375
- w_down: bfloat16 [1024, 256], replicated, may hold values from -0.1875 to 0.1875
Outputs:
- d_tokens: bfloat16 [128, 256, 256], P('rows', 'cols')
- d_gain_row: float32 [256], replicated
- d_w_qkv_row: float32 [256, 768], replicated
- d_w_out_row: float32 [256, 256], replicated
- d_gain_col: float32 [256], replicated
- d_w_qkv_col: float32 [256, 768], replicated
- d_w_out_col: float32 [256, 256], replicated
- d_gain_mlp: float32 [256], replicated
- d_w_up: float32 [256, 1024], replicated
- d_w_down: float32 [1024, 256], replicated
All inputs are finite; a program needn't handle non-finite values.
Results may differ from a plain program's by a relative error of at most 0.015.
Values may be sent and summed in bfloat16 or wider, within the bound.
No kernel may reach another device: no remote copies, remote signals or barrier semaphores. Data moves between devices by JAX's collectives and lax.ppermute only.
A program may use at most 128 MiB of HBM per device.

v0:
```python
import jax
import jax.numpy as jnp
from jax import lax
from jax.sharding import PartitionSpec as P

HEADS = 4


def product(spec_text, left_op, right_op):
    return jnp.einsum(spec_text, left_op, right_op, preferred_element_type=jnp.float32)


def layer_norm(entries, gain_vec):
    floats = entries.astype(jnp.float32)
    centred = floats - jnp.mean(floats, axis=-1, keepdims=True)
    inverse = lax.rsqrt(jnp.mean(centred * centred, axis=-1, keepdims=True) + 1e-05)
    normed = centred * inverse
    return ((normed * gain_vec).astype(jnp.bfloat16), normed, inverse)


def norm_back(grad_out, normed, inverse, gain_vec):
    scaled = grad_out * gain_vec
    result = inverse * (
        scaled
        - jnp.mean(scaled, axis=-1, keepdims=True)
        - normed * jnp.mean(scaled * normed, axis=-1, keepdims=True)
    )
    gain_grad = jnp.sum((grad_out * normed).reshape(-1, gain_vec.shape[0]), axis=0)
    return (result, gain_grad)


def over_cells(left_op, right_op):
    left_flat = left_op.reshape(-1, left_op.shape[-1])
    right_flat = right_op.reshape(-1, right_op.shape[-1])
    return lax.dot_general(
        left_flat, right_flat, (((0,), (0,)), ((), ())), preferred_element_type=jnp.float32
    )


def times_transpose(entries, weight):
    return lax.dot_general(
        entries, weight, (((entries.ndim - 1,), (1,)), ((), ())), preferred_element_type=jnp.float32
    )


def letters(length_axis):
    if length_axis == 1:
        return ("sqhd,skhd->shqk", "shqk,skhd->sqhd", "shqk,sqhd->skhd")
    return ("qshd,kshd->shqk", "shqk,kshd->qshd", "shqk,qshd->kshd")


def split_heads(packed, head_count):
    features = packed.shape[-1] // 3
    head_shape = packed.shape[:-1] + (head_count, features // head_count)
    return tuple(
        (
            packed[..., member * features : (member + 1) * features].reshape(head_shape)
            for member in range(3)
        )
    )


def key_terms(bias_rows, length_axis):
    floats = bias_rows.astype(jnp.float32)
    if length_axis == 0:
        floats = floats.T
    return floats[:, None, None, :]


def attention_weights(query_block, key_rows, bias_terms, factor, length_axis):
    scores = product(letters(length_axis)[0], query_block, key_rows) * factor + bias_terms
    shifted = jnp.exp(scores - jnp.max(scores, axis=-1, keepdims=True))
    return shifted / jnp.sum(shifted, axis=-1, keepdims=True)


def join_blocks(stacked, length_axis, features):
    if length_axis == 0:
        return stacked.reshape((-1, stacked.shape[2], features))
    reordered = jnp.moveaxis(stacked, 0, 1)
    return reordered.reshape((reordered.shape[0], -1, features))


def attend(packed, bias_rows, head_count, length_axis):
    query_rows, key_rows, value_rows = split_heads(packed, head_count)
    length = packed.shape[length_axis]
    block_len = min(length, 512)
    factor = query_rows.shape[-1] ** (-0.5)
    bias_terms = key_terms(bias_rows, length_axis)
    mixing = letters(length_axis)[1]

    def one_block(offset):
        query_block = lax.dynamic_slice_in_dim(query_rows, offset, block_len, length_axis)
        weights = attention_weights(query_block, key_rows, bias_terms, factor, length_axis)
        return product(mixing, weights.astype(jnp.bfloat16), value_rows).astype(jnp.bfloat16)

    offsets = jnp.arange(length // block_len, dtype=jnp.int32) * block_len
    return join_blocks(lax.map(one_block, offsets), length_axis, packed.shape[-1] // 3)


def attend_back(grad_out, packed, bias_rows, head_count, length_axis):
    query_rows, key_rows, value_rows = split_heads(packed, head_count)
    features = packed.shape[-1] // 3
    grad_heads = grad_out.reshape(query_rows.shape)
    length = packed.shape[length_axis]
    block_len = min(length, 512)
    factor = query_rows.shape[-1] ** (-0.5)
    bias_terms = key_terms(bias_rows, length_axis)
    score_spec, mixing, gather_spec = letters(length_axis)

    def one_block(running, offset):
        key_grad, value_grad = running
        query_block = lax.dynamic_slice_in_dim(query_rows, offset, block_len, length_axis)
        grad_block = lax.dynamic_slice_in_dim(grad_heads, offset, block_len, length_axis)
        weights = attention_weights(query_block, key_rows, bias_terms, factor, length_axis)
        weights_low = weights.astype(jnp.bfloat16)
        weight_grad = product(score_spec, grad_block, value_rows)
        centre = jnp.sum(weights * weight_grad, axis=-1, keepdims=True)
        score_grad = (weights * (weight_grad - centre) * factor).astype(jnp.bfloat16)
        query_grad = product(mixing, score_grad, key_rows)
        key_grad = key_grad + product(gather_spec, score_grad, query_block)
        value_grad = value_grad + product(gather_spec, weights_low, grad_block)
        return ((key_grad, value_grad), query_grad)

    empty_grad = jnp.zeros(key_rows.shape, jnp.float32)
    offsets = jnp.arange(length // block_len, dtype=jnp.int32) * block_len
    (key_grad, value_grad), query_parts = lax.scan(one_block, (empty_grad, empty_grad), offsets)
    query_grad = join_blocks(query_parts, length_axis, features)
    flat_shape = packed.shape[:-1] + (features,)
    joined = jnp.concatenate(
        [query_grad, key_grad.reshape(flat_shape), value_grad.reshape(flat_shape)], axis=-1
    )
    return joined.astype(jnp.bfloat16)


def attention_forward(inputs, bias_rows, gain_vec, w_qkv, w_out, head_count, length_axis):
    normal_in, normed, inverse = layer_norm(inputs, gain_vec)
    packed = jnp.dot(normal_in, w_qkv, preferred_element_type=jnp.float32).astype(jnp.bfloat16)
    mixed_out = attend(packed, bias_rows, head_count, length_axis)
    output = (
        inputs.astype(jnp.float32) + jnp.dot(mixed_out, w_out, preferred_element_type=jnp.float32)
    ).astype(jnp.bfloat16)
    return (output, (normal_in, normed, inverse, packed, mixed_out))


def attention_backward(
    grad_out, saved_parts, bias_rows, gain_vec, w_qkv, w_out, head_count, length_axis
):
    normal_in, normed, inverse, packed, mixed_out = saved_parts
    out_grad = over_cells(mixed_out, grad_out)
    mixed_grad = times_transpose(grad_out, w_out).astype(jnp.bfloat16)
    packed_grad = attend_back(mixed_grad, packed, bias_rows, head_count, length_axis)
    qkv_grad = over_cells(normal_in, packed_grad)
    input_grad, gain_grad = norm_back(
        times_transpose(packed_grad, w_qkv), normed, inverse, gain_vec
    )
    return (
        (grad_out.astype(jnp.float32) + input_grad).astype(jnp.bfloat16),
        (gain_grad, qkv_grad, out_grad),
    )


def feed_backward(inputs, grad_out, gain_vec, w_up, w_down):
    normal_in, normed, inverse = layer_norm(inputs, gain_vec)
    hidden = jnp.dot(normal_in, w_up, preferred_element_type=jnp.float32)
    active, gelu_back = jax.vjp(jax.nn.gelu, hidden)
    active_low = active.astype(jnp.bfloat16)
    down_grad = over_cells(active_low, grad_out)
    hidden_grad = gelu_back(times_transpose(grad_out, w_down))[0].astype(jnp.bfloat16)
    up_grad = over_cells(normal_in, hidden_grad)
    input_grad, gain_grad = norm_back(times_transpose(hidden_grad, w_up), normed, inverse, gain_vec)
    return (
        (grad_out.astype(jnp.float32) + input_grad).astype(jnp.bfloat16),
        (gain_grad, up_grad, down_grad),
    )


def shards(
    tokens,
    key_bias,
    cotangent,
    gain_row,
    w_qkv_row,
    w_out_row,
    gain_col,
    w_qkv_col,
    w_out_col,
    gain_mlp,
    w_up,
    w_down,
):
    row_cells, row_bias = (
        lax.all_to_all(tokens, "cols", split_axis=0, concat_axis=1, tiled=True),
        lax.all_to_all(key_bias, "cols", split_axis=0, concat_axis=1, tiled=True),
    )
    after_rows, row_saved = attention_forward(
        row_cells, row_bias, gain_row, w_qkv_row, w_out_row, HEADS, 1
    )
    column_cells = lax.all_to_all(
        lax.all_to_all(after_rows, "cols", split_axis=1, concat_axis=0, tiled=True),
        "rows",
        split_axis=1,
        concat_axis=0,
        tiled=True,
    )
    column_grads, column_bias = (
        lax.all_to_all(cotangent, "rows", split_axis=1, concat_axis=0, tiled=True),
        lax.all_to_all(key_bias, "rows", split_axis=1, concat_axis=0, tiled=True),
    )
    after_cols, column_saved = attention_forward(
        column_cells, column_bias, gain_col, w_qkv_col, w_out_col, HEADS, 0
    )
    mid_grad, feed_grads = feed_backward(after_cols, column_grads, gain_mlp, w_up, w_down)
    cell_grad, attn_grads = attention_backward(
        mid_grad, column_saved, column_bias, gain_col, w_qkv_col, w_out_col, HEADS, 0
    )
    factor = float(
        tokens.shape[0] * tokens.shape[1] * lax.axis_size("rows") * lax.axis_size("cols")
    ) ** (-0.5)
    other_sums = tuple((grad_term * factor for grad_term in attn_grads + feed_grads))
    grad_rows = lax.all_to_all(
        lax.all_to_all(cell_grad, "rows", split_axis=0, concat_axis=1, tiled=True),
        "cols",
        split_axis=0,
        concat_axis=1,
        tiled=True,
    )
    token_grad_rows, row_grads = attention_backward(
        grad_rows, row_saved, row_bias, gain_row, w_qkv_row, w_out_row, HEADS, 1
    )
    d_tokens = lax.all_to_all(token_grad_rows, "cols", split_axis=1, concat_axis=0, tiled=True)
    row_sums = tuple((grad_term * factor for grad_term in row_grads))
    summed = lax.psum(
        (
            row_sums[0],
            row_sums[1],
            row_sums[2],
            other_sums[0],
            other_sums[1],
            other_sums[2],
            other_sums[3],
            other_sums[4],
            other_sums[5],
        ),
        ("rows", "cols"),
    )
    row_sums = summed[:3]
    other_sums = summed[3:]
    return (
        d_tokens,
        row_sums[0],
        row_sums[1],
        row_sums[2],
        other_sums[0],
        other_sums[1],
        other_sums[2],
        other_sums[3],
        other_sums[4],
        other_sums[5],
    )


def solution(mesh):
    in_specs = (
        P("rows", "cols", None),
        P("rows", "cols"),
        P("rows", "cols", None),
        P(),
        P(),
        P(),
        P(),
        P(),
        P(),
        P(),
        P(),
        P(),
    )
    out_specs = (P("rows", "cols", None), P(), P(), P(), P(), P(), P(), P(), P(), P())
    return jax.shard_map(shards, mesh=mesh, in_specs=in_specs, out_specs=out_specs, check_vma=False)
```

profile of v0, /device:TPU:0, one launch (start us, length us, event | category | flops | bytes accessed | tf_op | source)
XLA Modules:
  0.0 385.8 jit_solution(3843586543527307721)
XLA Ops:
  7.2 12.1 %all_to_all.134 = bf16[8,4,32]{2,1,0:T(4,128)(2,1)S(1)} all-to-all(bf16[8,4,32]{2,1,0:T(4,128)(2,1)} %bitcast.263), channel_id=1, replica_groups=mesh['rows'=4,'cols'=8] {'cols'}, dimensions={0} | all-to-all | bytes 4096 | tf_op jit(solution)/shard_map/all_to_all | solution.py:193
  19.3 3.6 all-to-all-start.1
  24.4 13.7 %all-to-all-done.1 = bf16[32,32,256]{2,1,0:T(8,128)(2,1)S(1)} async-done(((bf16[32,32,256]{2,1,0:T(8,128)(2,1)}), bf16[32,32,256]{2,1,0:T(8,128)(2,1)S(1)}, u32[]{:S(2)}, u32[]{:S(2)}) %all-to-all-start.1) | async-done | bytes 524320 | tf_op jit(solution)/shard_map/all_to_all | solution.py:192
  38.2 3.7 all-to-all-start.5
  46.3 4.7 %fusion.124 = (f32[4,4,256]{2,1,0:T(4,128)S(1)}, f32[4,4,256,256]{2,3,1,0:T(8,128)}) fusion(f32[4,256]{1,0:T(4,128)S(1)} %reshape.252, bf16[4,256,4,64]{1,3,2,0:T(8,128)(2,1)S(1)} %bitcast.249, bf16[4,256,4,64]{1,3,2,0:T(8,128)(2,1)} %bitcast.247), kind=kOutput, calls=%fused_computation.165 | convolution fusion | flops 138412288 | bytes 5263360 | tf_op jit(solution)/shard_map/while/body/eval_jaxpr/sub | solution.py:72
  51.0 2.7 convolution_convert_fusion.7
  56.1 3.5 all-to-all-start.3
  60.7 14.2 %all-to-all-done.3 = bf16[4,256,256]{2,0,1:T(4,128)(2,1)S(1)} async-done(((bf16[4,256,256]{2,0,1:T(4,128)(2,1)}), bf16[4,256,256]{2,0,1:T(4,128)(2,1)S(1)}, u32[]{:S(2)}, u32[]{:S(2)}) %all-to-all-start.3) | async-done | bytes 524320 | tf_op jit(solution)/shard_map/all_to_all | solution.py:199
  74.8 4.2 %all-to-all-start = ((bf16[32,32,256]{2,0,1:T(8,128)(2,1)}), bf16[32,32,256]{2,0,1:T(8,128)(2,1)S(1)}, u32[]{:S(2)}, u32[]{:S(2)}) async-start(bf16[32,32,256]{2,0,1:T(8,128)(2,1)} %copy.364), calls=%async_computation | async-start | bytes 1048576 | tf_op jit(solution)/shard_map/all_to_all | solution.py:206
  80.2 6.6 %all-to-all-done = bf16[32,32,256]{2,0,1:T(8,128)(2,1)S(1)} async-done(((bf16[32,32,256]{2,0,1:T(8,128)(2,1)}), bf16[32,32,256]{2,0,1:T(8,128)(2,1)S(1)}, u32[]{:S(2)}, u32[]{:S(2)}) %all-to-all-start) | async-done | bytes 524320 | tf_op jit(solution)/shard_map/all_to_all | solution.py:206
  86.9 3.7 all-to-all-start.4
  91.5 5.8 %all-to-all-done.4 = bf16[32,32,256]{2,0,1:T(8,128)(2,1)S(1)} async-done(((bf16[32,32,256]{2,0,1:T(8,128)(2,1)}), bf16[32,32,256]{2,0,1:T(8,128)(2,1)S(1)}, u32[]{:S(2)}, u32[]{:S(2)}) %all-to-all-start.4) | async-done | bytes 524320 | tf_op jit(solution)/shard_map/all_to_all | solution.py:198
  107.9 3.7 fusion.125
  115.3 2.8 multiply_convert_fusion
  118.2 3.2 fusion.10
  127.3 3.5 convolution_convert_fusion.5
  132.6 5.2 %fusion.42 = bf16[8,4,64,128]{3,2,1,0:T(8,128)(2,1)} fusion(bf16[128,8,4,64]{0,3,2,1:T(8,128)(2,1)} %bitcast.252, f32[8,4,128,128]{2,3,1,0:T(8,128)} %fusion.126, f32[8,4,128,128]{2,3,1,0:T(8,128)} %get-tuple-element.127, f32[8,4,128]{2,1,0:T(4,128)S(1)} %get-tuple-element.126), kind=kOutput, calls=%fused_computation.49 | convolution fusion | flops 71045248 | bytes 5259264 | tf_op jit(solution)/shard_map/while/body/eval_jaxpr/shqk,kshd->qshd/dot_general | solution.py:10
  137.9 5.0 %fusion.45 = bf16[8,4,64,128]{3,2,1,0:T(8,128)(2,1)} fusion(bf16[128,8,4,64]{0,3,2,1:T(8,128)(2,1)S(1)} %bitcast.254, f32[8,4,128,128]{2,3,1,0:T(8,128)} %fusion.126, f32[8,4,128,128]{2,3,1,0:T(8,128)} %get-tuple-element.127, f32[8,4,128]{2,1,0:T(4,128)S(1)} %get-tuple-element.126), kind=kOutput, calls=%fused_computation.50 | convolution fusion | flops 71045248 | bytes 5259264 | tf_op jit(solution)/shard_map/while/body/eval_jaxpr/shqk,qshd->kshd/dot_general | solution.py:10
  148.4 3.2 multiply_reduce_fusion.2
  153.6 4.1 %all-to-all-start.6 = ((bf16[128,8,256]{2,1,0:T(8,128)(2,1)}), bf16[128,8,256]{2,1,0:T(8,128)(2,1)}, u32[]{:S(2)}, u32[]{:S(2)}) async-start(bf16[128,8,256]{2,1,0:T(8,128)(2,1)} %copy.399), calls=%async_computation.6 | async-start | bytes 1048576 | tf_op jit(solution)/shard_map/all_to_all | solution.py:221
  166.3 3.5 all-to-all-start.7
  172.3 3.0 fusion.56
  177.3 2.4 fusion.39
  179.7 5.3 %all-to-all-done.7 = bf16[32,32,256]{2,1,0:T(8,128)(2,1)S(1)} async-done(((bf16[32,32,256]{2,1,0:T(8,128)(2,1)}), bf16[32,32,256]{2,1,0:T(8,128)(2,1)S(1)}, u32[]{:S(2)}, u32[]{:S(2)}) %all-to-all-start.7) | async-done | bytes 524320 | tf_op jit(solution)/shard_map/all_to_all | solution.py:220
  185.4 3.8 convolution_convert_fusion.4
  189.3 2.7 fusion.127
  192.0 8.0 %fusion.48 = bf16[4,4,64,256]{3,2,1,0:T(8,128)(2,1)} fusion(bf16[4,256,4,64]{1,3,2,0:T(8,128)(2,1)S(1)} %bitcast.248, f32[4,4,256,256]{2,3,1,0:T(8,128)} %fusion.127, f32[4,4,256,256]{2,3,1,0:T(8,128)} %get-tuple-element.125, f32[4,4,256]{2,1,0:T(4,128)S(1)} %get-tuple-element.124), kind=kOutput, calls=%fused_computation.51 | convolution fusion | flops 141824256 | bytes 9453568 | tf_op jit(solution)/shard_map/while/body/eval_jaxpr/shqk,skhd->sqhd/dot_general | solution.py:10
  200.0 8.0 %fusion.51 = bf16[4,4,64,256]{3,2,1,0:T(8,128)(2,1)} fusion(bf16[4,256,4,64]{1,3,2,0:T(8,128)(2,1)S(1)} %bitcast.250, f32[4,4,256,256]{2,3,1,0:T(8,128)} %fusion.127, f32[4,4,256,256]{2,3,1,0:T(8,128)} %get-tuple-element.125, f32[4,4,256]{2,1,0:T(4,128)S(1)} %get-tuple-element.124), kind=kOutput, calls=%fused_computation.52 | convolution fusion | flops 141824256 | bytes 9453568 | tf_op jit(solution)/shard_map/while/body/eval_jaxpr/shqk,sqhd->skhd/dot_general | solution.py:10
  214.5 2.7 fusion.57
  221.9 3.5 all-to-all-start.8
  225.4 41.2 %all-reduce = (f32[256]{0:T(256)}, f32[256]{0:T(256)}, f32[256]{0:T(256)}) all-reduce(f32[256]{0:T(256)S(1)} %broadcast_multiply_fusion.11, f32[256]{0:T(256)S(1)} %broadcast_multiply_fusion.10, f32[256]{0:T(256)S(1)} %broadcast_multiply_fusion.9), channel_id=1, replica_groups=mesh['rows'=4,'cols'=8] {'rows','cols'}, use_global_device_ids=true, to_apply=%region_19.20 | all-reduce | flops 768 | bytes 6144 | tf_op jit(solution)/shard_map/psum | solution.py:232
  267.6 102.7 %all-reduce.4.cloned.1.call-done = (f32[256,768]{1,0:T(8,128)}, f32[256,256]{1,0:T(8,128)}, f32[256,768]{1,0:T(8,128)}, f32[256,256]{1,0:T(8,128)}, f32[256,1024]{1,0:T(8,128)}, /*index=5*/f32[1024,256]{1,0:T(8,128)}) async-done(((f32[256,768]{1,0:T(8,128)}, f32[256,256]{1,0:T(8,128)}, f32[256,768]{1,0:T(8,128)}, f32[256,256]{1,0:T(8,128)}, f32[256,1024]{1,0:T(8,128)}, /*index=5*/f32[1024,256]{1,0:T(8,128)}), ...) | async-done | bytes 4194320 | tf_op jit(solution)/shard_map/psum | solution.py:232
  (194 shorter events, 75.1 us)
Async XLA Ops:
  7.2 108.1 %copy-start = (bf16[256,1024]{1,0:T(8,128)(2,1)S(1)}, bf16[256,1024]{1,0:T(8,128)(2,1)}, u32[]{:S(2)}) copy-start(bf16[256,1024]{1,0:T(8,128)(2,1)} %param.22) | copy-start | bytes 1572868
  19.3 23.7 %copy-start.41 = (f32[256]{0:T(256)S(1)}, f32[256]{0:T(256)}, u32[]{:S(2)}) copy-start(f32[256]{0:T(256)} %param.15) | copy-start | bytes 3076
  19.3 18.9 %all-to-all-start.1 = ((bf16[32,32,256]{2,1,0:T(8,128)(2,1)}), bf16[32,32,256]{2,1,0:T(8,128)(2,1)S(1)}, u32[]{:S(2)}, u32[]{:S(2)}) async-start(bf16[32,32,256]{2,1,0:T(8,128)(2,1)} %param.12), calls=%async_computation.1 | async-start | bytes 1048576 | tf_op jit(solution)/shard_map/all_to_all | solution.py:192
  38.2 17.9 %all-to-all-start.5 = ((bf16[4,2,128]{2,1,0:T(2,128)(2,1)}), bf16[4,2,128]{2,1,0:T(2,128)(2,1)S(1)}, u32[]{:S(2)}, u32[]{:S(2)}) async-start(bf16[4,2,128]{2,1,0:T(2,128)(2,1)} %reshape.268), calls=%async_computation.5 | async-start | bytes 4096 | tf_op jit(solution)/shard_map/all_to_all | solution.py:207
  46.0 4.9 %copy-start.29 = (bf16[4,256,256]{1,2,0:T(8,128)(2,1)}, bf16[4,256,256]{1,2,0:T(8,128)(2,1)S(1)}, u32[]{:S(2)}) copy-start(bf16[4,256,256]{1,2,0:T(8,128)(2,1)S(1)} %copy.369) | copy-start | bytes 1572868
  46.2 4.7 %copy-start.8 = (bf16[4,256,256]{1,2,0:T(8,128)(2,1)}, bf16[4,256,256]{1,2,0:T(8,128)(2,1)S(1)}, u32[]{:S(2)}) copy-start(bf16[4,256,256]{1,2,0:T(8,128)(2,1)S(1)} %copy.368) | copy-start | bytes 1572868
  53.7 5.9 %copy-start.27 = (bf16[32,32,256]{2,1,0:T(8,128)(2,1)S(1)}, bf16[32,32,256]{2,1,0:T(8,128)(2,1)}, u32[]{:S(2)}) copy-start(bf16[32,32,256]{2,1,0:T(8,128)(2,1)} %param.14) | copy-start | bytes 1572868
  56.1 18.8 %all-to-all-start.3 = ((bf16[4,256,256]{2,0,1:T(4,128)(2,1)}), bf16[4,256,256]{2,0,1:T(4,128)(2,1)S(1)}, u32[]{:S(2)}, u32[]{:S(2)}) async-start(bf16[4,256,256]{2,0,1:T(4,128)(2,1)} %copy.374), calls=%async_computation.3 | async-start | bytes 1048576 | tf_op jit(solution)/shard_map/all_to_all | solution.py:199
  74.8 12.0 %all-to-all-start = ((bf16[32,32,256]{2,0,1:T(8,128)(2,1)}), bf16[32,32,256]{2,0,1:T(8,128)(2,1)S(1)}, u32[]{:S(2)}, u32[]{:S(2)}) async-start(bf16[32,32,256]{2,0,1:T(8,128)(2,1)} %copy.364), calls=%async_computation | async-start | bytes 1048576 | tf_op jit(solution)/shard_map/all_to_all | solution.py:206
  86.9 11.8 %copy-start.2 = (bf16[32,32,256]{2,0,1:T(8,128)(2,1)}, bf16[32,32,256]{2,0,1:T(8,128)(2,1)S(1)}, u32[]{:S(2)}) copy-start(bf16[32,32,256]{2,0,1:T(8,128)(2,1)S(1)} %all-to-all-done) | copy-start | bytes 1572868
  86.9 10.4 %all-to-all-start.4 = ((bf16[32,32,256]{2,0,1:T(8,128)(2,1)}), bf16[32,32,256]{2,0,1:T(8,128)(2,1)S(1)}, u32[]{:S(2)}, u32[]{:S(2)}) async-start(bf16[32,32,256]{2,0,1:T(8,128)(2,1)} %copy.377), calls=%async_computation.4 | async-start | bytes 1048576 | tf_op jit(solution)/shard_map/all_to_all | solution.py:198
  90.7 8.9 %copy-start.40 = (f32[256]{0:T(256)S(1)}, f32[256]{0:T(256)}, u32[]{:S(2)}) copy-start(f32[256]{0:T(256)} %param.18) | copy-start | bytes 3076
  107.9 5.8 %copy-start.20 = (bf16[128,8,256]{0,2,1:T(8,128)(2,1)}, bf16[128,8,256]{0,2,1:T(8,128)(2,1)S(1)}, u32[]{:S(2)}) copy-start(bf16[128,8,256]{0,2,1:T(8,128)(2,1)S(1)} %copy.385) | copy-start | bytes 1572868
  132.6 5.2 %copy-start.32 = (bf16[128,8,256]{0,2,1:T(8,128)(2,1)S(1)}, bf16[128,8,256]{0,2,1:T(8,128)(2,1)}, u32[]{:S(2)}) copy-start(bf16[128,8,256]{0,2,1:T(8,128)(2,1)} %copy.386) | copy-start | bytes 1572868
  144.1 4.3 %copy-start.31 = (bf16[128,8,256]{2,0,1:T(8,128)(2,1)}, bf16[128,8,256]{2,0,1:T(8,128)(2,1)S(1)}, u32[]{:S(2)}) copy-start(bf16[128,8,256]{2,0,1:T(8,128)(2,1)S(1)} %copy.398) | copy-start | bytes 1572868
  151.6 6.1 %copy-start.3 = (bf16[32,32,256]{2,0,1:T(8,128)(2,1)S(1)}, bf16[32,32,256]{2,0,1:T(8,128)(2,1)}, u32[]{:S(2)}) copy-start(bf16[32,32,256]{2,0,1:T(8,128)(2,1)} %copy-done.2) | copy-start | bytes 1572868
  152.5 6.3 %copy-start.11 = (bf16[4,4,64,256]{3,2,1,0:T(8,128)(2,1)S(1)}, bf16[4,4,64,256]{3,2,1,0:T(8,128)(2,1)}, u32[]{:S(2)}) copy-start(bf16[4,4,64,256]{3,2,1,0:T(8,128)(2,1)} %copy-done.10) | copy-start | bytes 1572868
  153.6 10.8 %all-to-all-start.6 = ((bf16[128,8,256]{2,1,0:T(8,128)(2,1)}), bf16[128,8,256]{2,1,0:T(8,128)(2,1)}, u32[]{:S(2)}, u32[]{:S(2)}) async-start(bf16[128,8,256]{2,1,0:T(8,128)(2,1)} %copy.399), calls=%async_computation.6 | async-start | bytes 1048576 | tf_op jit(solution)/shard_map/all_to_all | solution.py:221
  159.2 10.9 %copy-start.6 = (bf16[128,8,256]{2,0,1:T(8,128)(2,1)S(1)}, bf16[128,8,256]{2,0,1:T(8,128)(2,1)}, u32[]{:S(2)}) copy-start(bf16[128,8,256]{2,0,1:T(8,128)(2,1)} %copy-done.4) | copy-start | bytes 1572868
  163.5 8.9 %copy-start.18 = (bf16[128,8,256]{2,0,1:T(8,128)(2,1)S(1)}, bf16[128,8,256]{2,0,1:T(8,128)(2,1)}, u32[]{:S(2)}) copy-start(bf16[128,8,256]{2,0,1:T(8,128)(2,1)} %copy-done.17) | copy-start | bytes 1572868
  166.3 18.8 %all-to-all-start.7 = ((bf16[32,32,256]{2,1,0:T(8,128)(2,1)}), bf16[32,32,256]{2,1,0:T(8,128)(2,1)S(1)}, u32[]{:S(2)}, u32[]{:S(2)}) async-start(bf16[32,32,256]{2,1,0:T(8,128)(2,1)} %bitcast.239), calls=%async_computation.7 | async-start | bytes 1048576 | tf_op jit(solution)/shard_map/all_to_all | solution.py:220
  169.8 200.5 %all-reduce.4.cloned.1.call-start = ((), (), s32[]{:S(2)}) async-start(), calls=%async_computation.9 | async-start | bytes 8388608 | tf_op jit(solution)/shard_map/psum | solution.py:232
  192.0 8.0 %copy-start.30 = (bf16[4,256,256]{1,2,0:T(8,128)(2,1)S(1)}, bf16[4,256,256]{1,2,0:T(8,128)(2,1)}, u32[]{:S(2)}) copy-start(bf16[4,256,256]{1,2,0:T(8,128)(2,1)} %copy-done.29) | copy-start | bytes 1572868
  208.0 5.5 %copy-start.19 = (bf16[32,8,4,256]{3,1,2,0:T(8,128)(2,1)S(1)}, bf16[32,8,4,256]{3,1,2,0:T(8,128)(2,1)}, u32[]{:S(2)}) copy-start(bf16[32,8,4,256]{3,1,2,0:T(8,128)(2,1)} %copy.437) | copy-start | bytes 1572868
  208.0 6.5 %copy-start.16 = (bf16[4,256,256]{2,1,0:T(8,128)(2,1)S(1)}, bf16[4,256,256]{2,1,0:T(8,128)(2,1)}, u32[]{:S(2)}) copy-start(bf16[4,256,256]{2,1,0:T(8,128)(2,1)} %copy-done.15) | copy-start | bytes 1572868
  219.8 5.6 %copy-start.42 = (f32[256]{0:T(256)S(1)}, f32[256]{0:T(256)}, u32[]{:S(2)}) copy-start(f32[256]{0:T(256)} %get-tuple-element.73) | copy-start | bytes 3076
  219.8 5.6 %copy-start.43 = (f32[256]{0:T(256)S(1)}, f32[256]{0:T(256)}, u32[]{:S(2)}) copy-start(f32[256]{0:T(256)} %get-tuple-element.84) | copy-start | bytes 3076
  221.9 44.8 %all-to-all-start.8 = ((bf16[4,256,256]{2,0,1:T(4,128)(2,1)}), bf16[4,256,256]{2,0,1:T(4,128)(2,1)S(1)}, u32[]{:S(2)}, u32[]{:S(2)}) async-start(bf16[4,256,256]{2,0,1:T(4,128)(2,1)} %copy.409), calls=%async_computation.8 | async-start | bytes 1048576 | tf_op jit(solution)/shard_map/all_to_all | solution.py:230
  370.2 6.0 %copy-start.38 = (f32[256,256]{1,0:T(8,128)S(1)}, f32[256,256]{1,0:T(8,128)}, u32[]{:S(2)}) copy-start(f32[256,256]{1,0:T(8,128)} %get-tuple-element.143) | copy-start | bytes 786436
  370.2 6.7 %copy-start.24 = (f32[256,1024]{1,0:T(8,128)S(1)}, f32[256,1024]{1,0:T(8,128)}, u32[]{:S(2)}) copy-start(f32[256,1024]{1,0:T(8,128)} %get-tuple-element.145) | copy-start | bytes 3145732
  370.2 7.7 %copy-start.23 = (f32[1024,256]{1,0:T(8,128)S(1)}, f32[1024,256]{1,0:T(8,128)}, u32[]{:S(2)}) copy-start(f32[1024,256]{1,0:T(8,128)} %get-tuple-element.146) | copy-start | bytes 3145732
  372.5 6.4 %copy-start.1 = (bf16[256,1024]{1,0:T(8,128)(2,1)S(1)}, bf16[256,1024]{1,0:T(8,128)(2,1)}, u32[]{:S(2)}) copy-start(bf16[256,1024]{1,0:T(8,128)(2,1)} %param.22) | copy-start | bytes 1572868
  (23 other events, 51.3 us)
Sparse Core Ops, SparseCore 0:
  217.3 152.8 all-reduce.3
where the time goes:
time: 387 us; the launch traced here: 386 us
  waiting for transfers between devices  149 us (39%)
  matrix products  80.4 us (21%)
  blocking collectives  53.3 us (14%)
  local copies, waits for them, and re-layouts  52.3 us (14%)
  starting transfers between devices  30.1 us (8%)
  between operations  14.7 us (4%)
  other arithmetic  5.81 us (2%)
    psum x1, waiting for transfers between devices, shards(): lax.psum((row_sums[0], row_sums[1], row_sums[2], other_sums[0], other_sum...  103 us
    dot_general x10, matrix products, product(): jnp.einsum(spec_text, left_op, right_op, preferred_element_type=jnp.float32)  42.8 us
    psum x1, blocking collectives, shards(): lax.psum((row_sums[0], row_sums[1], row_sums[2], other_sums[0], other_sum...  41.2 us
    unnamed x104, local copies, waits for them, and re-layouts  17.6 us
    all_to_all x1, waiting for transfers between devices, shards(): lax.all_to_all(after_rows, 'cols', split_axis=1, concat_axis=0, tiled=True)  14.2 us
    all_to_all x1, waiting for transfers between devices, shards(): lax.all_to_all(tokens, 'cols', split_axis=0, concat_axis=1, tiled=True)  13.7 us
    dot_general x6, matrix products, over_cells(): lax.dot_general(left_flat, right_flat, (((0,), (0,)), ((), ())), preferre...  13.3 us
    all_to_all x1, blocking collectives, shards(): lax.all_to_all(key_bias, 'cols', split_axis=0, concat_axis=1, tiled=True)  12.1 us
  transfers between devices with their start and end apart: 9, of which 7 were waited for; matrix products, arithmetic and copies ran while one was open for 10% of the time, Pallas kernels for 0%

commit v1 on v0

--- a/solution.py
+++ b/solution.py
@@ -230,18 +230,21 @@
     d_tokens = lax.all_to_all(token_grad_rows, "cols", split_axis=1, concat_axis=0, tiled=True)
     row_sums = tuple((grad_term * factor for grad_term in row_grads))
     summed = lax.psum(
-        (
-            row_sums[0],
-            row_sums[1],
-            row_sums[2],
-            other_sums[0],
-            other_sums[1],
-            other_sums[2],
-            other_sums[3],
-            other_sums[4],
-            other_sums[5],
+        lax.psum(
+            (
+                row_sums[0],
+                row_sums[1],
+                row_sums[2],
+                other_sums[0],
+                other_sums[1],
+                other_sums[2],
+                other_sums[3],
+                other_sums[4],
+                other_sums[5],
+            ),
+            "cols",
         ),
-        ("rows", "cols"),
+        "rows",
     )
     row_sums = summed[:3]
     other_sums = summed[3:]

time: 387 us -> 442 us (1.14)
  waiting for transfers between devices: 149 us -> 214 us
  blocking collectives: 53.3 us -> 43.4 us
    psum x0 -> x1, waiting for transfers between devices: none -> 70.8 us  [shards(): lax.psum(lax.psum((row_sums[0], row_sums[1], row_sums[2], other_sums[0],...]
    psum x1, blocking collectives: 41.2 us -> 20.9 us  [shards(): lax.psum((row_sums[0], row_sums[1], row_sums[2], other_sums[0], other_sum...]
    psum x0 -> x1, blocking collectives: none -> 10.5 us  [shards(): lax.psum(lax.psum((row_sums[0], row_sums[1], row_sums[2], other_sums[0],...]
    psum x1, waiting for transfers between devices: 103 us -> 96.9 us  [shards(): lax.psum((row_sums[0], row_sums[1], row_sums[2], other_sums[0], other_sum...]
  transfers between devices with their start and end apart: 9 -> 10, of which waited for: 7 -> 8; matrix products, arithmetic and copies ran while one was open for 10% -> 8% of each run, Pallas kernels for 0% -> 0%
where the time goes in v1:
time: 442 us; the launch traced here: 440 us
  waiting for transfers between devices  214 us (48%)
  matrix products  80.5 us (18%)
  local copies, waits for them, and re-layouts  51 us (12%)
  blocking collectives  43.4 us (10%)
  starting transfers between devices  30.5 us (7%)
  between operations  14.7 us (3%)
  other arithmetic  5.81 us (1%)
    psum x1, waiting for transfers between devices, shards(): lax.psum((row_sums[0], row_sums[1], row_sums[2], other_sums[0], other_sum...  96.9 us
    psum x1, waiting for transfers between devices, shards(): lax.psum(lax.psum((row_sums[0], row_sums[1], row_sums[2], other_sums[0],...  70.8 us
    dot_general x10, matrix products, product(): jnp.einsum(spec_text, left_op, right_op, preferred_element_type=jnp.float32)  43 us
    psum x1, blocking collectives, shards(): lax.psum((row_sums[0], row_sums[1], row_sums[2], other_sums[0], other_sum...  20.9 us
    unnamed x104, local copies, waits for them, and re-layouts  16.3 us
    all_to_all x1, waiting for transfers between devices, shards(): lax.all_to_all(after_rows, 'cols', split_axis=1, concat_axis=0, tiled=True)  14.2 us
    all_to_all x1, waiting for transfers between devices, shards(): lax.all_to_all(tokens, 'cols', split_axis=0, concat_axis=1, tiled=True)  13.7 us
    dot_general x6, matrix products, over_cells(): lax.dot_general(left_flat, right_flat, (((0,), (0,)), ((), ())), preferre...  13.3 us
  transfers between devices with their start and end apart: 10, of which 8 were waited for; matrix products, arithmetic and copies ran while one was open for 8% of the time, Pallas kernels for 0%

profile of v1, /device:TPU:0, one launch (start us, length us, event | category | flops | bytes accessed | tf_op | source)
XLA Modules:
  0.0 440.2 jit_solution(9388503108146158370)
XLA Ops:
  7.2 12.1 %all_to_all.134 = bf16[8,4,32]{2,1,0:T(4,128)(2,1)S(1)} all-to-all(bf16[8,4,32]{2,1,0:T(4,128)(2,1)} %bitcast.263), channel_id=1, replica_groups=mesh['rows'=4,'cols'=8] {'cols'}, dimensions={0} | all-to-all | bytes 4096 | tf_op jit(solution)/shard_map/all_to_all | solution.py:193
  19.3 3.6 all-to-all-start.1
  24.4 13.7 %all-to-all-done.1 = bf16[32,32,256]{2,1,0:T(8,128)(2,1)S(1)} async-done(((bf16[32,32,256]{2,1,0:T(8,128)(2,1)}), bf16[32,32,256]{2,1,0:T(8,128)(2,1)S(1)}, u32[]{:S(2)}, u32[]{:S(2)}) %all-to-all-start.1) | async-done | bytes 524320 | tf_op jit(solution)/shard_map/all_to_all | solution.py:192
  38.2 3.7 all-to-all-start.5
  46.3 4.7 %fusion.124 = (f32[4,4,256]{2,1,0:T(4,128)S(1)}, f32[4,4,256,256]{2,3,1,0:T(8,128)}) fusion(f32[4,256]{1,0:T(4,128)S(1)} %reshape.252, bf16[4,256,4,64]{1,3,2,0:T(8,128)(2,1)S(1)} %bitcast.249, bf16[4,256,4,64]{1,3,2,0:T(8,128)(2,1)} %bitcast.247), kind=kOutput, calls=%fused_computation.165 | convolution fusion | flops 138412288 | bytes 5263360 | tf_op jit(solution)/shard_map/while/body/eval_jaxpr/sub | solution.py:72
  51.0 2.7 convolution_convert_fusion.7
  56.1 3.5 all-to-all-start.3
  60.7 14.2 %all-to-all-done.3 = bf16[4,256,256]{2,0,1:T(4,128)(2,1)S(1)} async-done(((bf16[4,256,256]{2,0,1:T(4,128)(2,1)}), bf16[4,256,256]{2,0,1:T(4,128)(2,1)S(1)}, u32[]{:S(2)}, u32[]{:S(2)}) %all-to-all-start.3) | async-done | bytes 524320 | tf_op jit(solution)/shard_map/all_to_all | solution.py:199
  74.8 4.2 all-to-all-start
  80.2 6.6 %all-to-all-done = bf16[32,32,256]{2,0,1:T(8,128)(2,1)S(1)} async-done(((bf16[32,32,256]{2,0,1:T(8,128)(2,1)}), bf16[32,32,256]{2,0,1:T(8,128)(2,1)S(1)}, u32[]{:S(2)}, u32[]{:S(2)}) %all-to-all-start) | async-done | bytes 524320 | tf_op jit(solution)/shard_map/all_to_all | solution.py:206
  86.9 3.7 all-to-all-start.4
  91.5 5.8 %all-to-all-done.4 = bf16[32,32,256]{2,0,1:T(8,128)(2,1)S(1)} async-done(((bf16[32,32,256]{2,0,1:T(8,128)(2,1)}), bf16[32,32,256]{2,0,1:T(8,128)(2,1)S(1)}, u32[]{:S(2)}, u32[]{:S(2)}) %all-to-all-start.4) | async-done | bytes 524320 | tf_op jit(solution)/shard_map/all_to_all | solution.py:198
  107.9 3.7 fusion.125
  115.3 2.8 multiply_convert_fusion
  118.2 3.2 fusion.10
  127.3 3.5 convolution_convert_fusion.5
  132.6 5.3 %fusion.42 = bf16[8,4,64,128]{3,2,1,0:T(8,128)(2,1)} fusion(bf16[128,8,4,64]{0,3,2,1:T(8,128)(2,1)} %bitcast.252, f32[8,4,128,128]{2,3,1,0:T(8,128)} %fusion.126, f32[8,4,128,128]{2,3,1,0:T(8,128)} %get-tuple-element.136, f32[8,4,128]{2,1,0:T(4,128)S(1)} %get-tuple-element.135), kind=kOutput, calls=%fused_computation.49 | convolution fusion | flops 71045248 | bytes 5259264 | tf_op jit(solution)/shard_map/while/body/eval_jaxpr/shqk,kshd->qshd/dot_general | solution.py:10
  137.9 5.0 %fusion.45 = bf16[8,4,64,128]{3,2,1,0:T(8,128)(2,1)} fusion(bf16[128,8,4,64]{0,3,2,1:T(8,128)(2,1)S(1)} %bitcast.254, f32[8,4,128,128]{2,3,1,0:T(8,128)} %fusion.126, f32[8,4,128,128]{2,3,1,0:T(8,128)} %get-tuple-element.136, f32[8,4,128]{2,1,0:T(4,128)S(1)} %get-tuple-element.135), kind=kOutput, calls=%fused_computation.50 | convolution fusion | flops 71045248 | bytes 5259264 | tf_op jit(solution)/shard_map/while/body/eval_jaxpr/shqk,qshd->kshd/dot_general | solution.py:10
  148.5 3.2 multiply_reduce_fusion.2
  153.6 4.1 all-to-all-start.6
  166.3 3.5 all-to-all-start.7
  172.4 3.0 fusion.56
  179.8 5.3 %all-to-all-done.7 = bf16[32,32,256]{2,1,0:T(8,128)(2,1)S(1)} async-done(((bf16[32,32,256]{2,1,0:T(8,128)(2,1)}), bf16[32,32,256]{2,1,0:T(8,128)(2,1)S(1)}, u32[]{:S(2)}, u32[]{:S(2)}) %all-to-all-start.7) | async-done | bytes 524320 | tf_op jit(solution)/shard_map/all_to_all | solution.py:220
  185.5 3.8 convolution_convert_fusion.4
  189.3 2.7 fusion.127
  192.0 8.1 %fusion.48 = bf16[4,4,64,256]{3,2,1,0:T(8,128)(2,1)} fusion(bf16[4,256,4,64]{1,3,2,0:T(8,128)(2,1)S(1)} %bitcast.248, f32[4,4,256,256]{2,3,1,0:T(8,128)} %fusion.127, f32[4,4,256,256]{2,3,1,0:T(8,128)} %get-tuple-element.134, f32[4,4,256]{2,1,0:T(4,128)S(1)} %get-tuple-element.133), kind=kOutput, calls=%fused_computation.51 | convolution fusion | flops 141824256 | bytes 9453568 | tf_op jit(solution)/shard_map/while/body/eval_jaxpr/shqk,skhd->sqhd/dot_general | solution.py:10
  200.1 8.0 %fusion.51 = bf16[4,4,64,256]{3,2,1,0:T(8,128)(2,1)} fusion(bf16[4,256,4,64]{1,3,2,0:T(8,128)(2,1)S(1)} %bitcast.250, f32[4,4,256,256]{2,3,1,0:T(8,128)} %fusion.127, f32[4,4,256,256]{2,3,1,0:T(8,128)} %get-tuple-element.134, f32[4,4,256]{2,1,0:T(4,128)S(1)} %get-tuple-element.133), kind=kOutput, calls=%fused_computation.52 | convolution fusion | flops 141824256 | bytes 9453568 | tf_op jit(solution)/shard_map/while/body/eval_jaxpr/shqk,sqhd->skhd/dot_general | solution.py:10
  217.3 96.9 %all-reduce.7.cloned.1.call-done = (f32[256,768]{1,0:T(8,128)}, f32[256,256]{1,0:T(8,128)}, f32[256,768]{1,0:T(8,128)}, f32[256,256]{1,0:T(8,128)}, f32[256,1024]{1,0:T(8,128)}, /*index=5*/f32[1024,256]{1,0:T(8,128)}) async-done(((f32[256,768]{1,0:T(8,128)}, f32[256,256]{1,0:T(8,128)}, f32[256,768]{1,0:T(8,128)}, f32[256,256]{1,0:T(8,128)}, f32[256,1024]{1,0:T(8,128)}, /*index=5*/f32[1024,256]{1,0:T(8,128)}), ...) | async-done | bytes 4194320 | tf_op jit(solution)/shard_map/psum | solution.py:233
  317.7 3.8 all-to-all-start.8
  321.6 20.9 %all-reduce = (f32[256]{0:T(256)S(1)}, f32[256]{0:T(256)S(1)}, f32[256]{0:T(256)S(1)}) all-reduce(f32[256]{0:T(256)S(1)} %broadcast_multiply_fusion.11, f32[256]{0:T(256)S(1)} %broadcast_multiply_fusion.10, f32[256]{0:T(256)S(1)} %broadcast_multiply_fusion.9), channel_id=1, replica_groups=mesh['rows'=4,'cols'=8] {'cols'}, use_global_device_ids=true, to_apply=%region_19.20 | all-reduce | flops 768 | bytes 6144 | tf_op jit(solution)/shard_map/psum | solution.py:233
  342.5 10.5 %all-reduce.2 = (f32[256]{0:T(256)}, f32[256]{0:T(256)}, f32[256]{0:T(256)}) all-reduce(f32[256]{0:T(256)S(1)} %get-tuple-element.91, f32[256]{0:T(256)S(1)} %get-tuple-element.92, f32[256]{0:T(256)S(1)} %get-tuple-element.102), channel_id=1, replica_groups=mesh['rows'=4,'cols'=8] {'rows'}, use_global_device_ids=true, to_apply=%region_20.21 | all-reduce | flops 768 | bytes 6144 | tf_op jit(solution)/shard_map/psum | solution.py:232
  353.9 70.8 %all-reduce.9.cloned.1.call-done = (f32[256,768]{1,0:T(8,128)}, f32[256,256]{1,0:T(8,128)}, f32[256,768]{1,0:T(8,128)}, f32[256,256]{1,0:T(8,128)}, f32[256,1024]{1,0:T(8,128)}, /*index=5*/f32[1024,256]{1,0:T(8,128)}) async-done(((f32[256,768]{1,0:T(8,128)}, f32[256,256]{1,0:T(8,128)}, f32[256,768]{1,0:T(8,128)}, f32[256,256]{1,0:T(8,128)}, f32[256,1024]{1,0:T(8,128)}, /*index=5*/f32[1024,256]{1,0:T(8,128)}), ...) | async-done | bytes 4194320 | tf_op jit(solution)/shard_map/psum | solution.py:232
  (198 shorter events, 78.9 us)
Async XLA Ops:
  7.2 108.1 %copy-start = (bf16[256,1024]{1,0:T(8,128)(2,1)S(1)}, bf16[256,1024]{1,0:T(8,128)(2,1)}, u32[]{:S(2)}) copy-start(bf16[256,1024]{1,0:T(8,128)(2,1)} %param.22) | copy-start | bytes 1572868
  19.3 23.7 %copy-start.41 = (f32[256]{0:T(256)S(1)}, f32[256]{0:T(256)}, u32[]{:S(2)}) copy-start(f32[256]{0:T(256)} %param.15) | copy-start | bytes 3076
  19.3 18.9 %all-to-all-start.1 = ((bf16[32,32,256]{2,1,0:T(8,128)(2,1)}), bf16[32,32,256]{2,1,0:T(8,128)(2,1)S(1)}, u32[]{:S(2)}, u32[]{:S(2)}) async-start(bf16[32,32,256]{2,1,0:T(8,128)(2,1)} %param.12), calls=%async_computation.1 | async-start | bytes 1048576 | tf_op jit(solution)/shard_map/all_to_all | solution.py:192
  38.2 17.9 %all-to-all-start.5 = ((bf16[4,2,128]{2,1,0:T(2,128)(2,1)}), bf16[4,2,128]{2,1,0:T(2,128)(2,1)S(1)}, u32[]{:S(2)}, u32[]{:S(2)}) async-start(bf16[4,2,128]{2,1,0:T(2,128)(2,1)} %reshape.268), calls=%async_computation.5 | async-start | bytes 4096 | tf_op jit(solution)/shard_map/all_to_all | solution.py:207
  53.7 5.9 %copy-start.27 = (bf16[32,32,256]{2,1,0:T(8,128)(2,1)S(1)}, bf16[32,32,256]{2,1,0:T(8,128)(2,1)}, u32[]{:S(2)}) copy-start(bf16[32,32,256]{2,1,0:T(8,128)(2,1)} %param.14) | copy-start | bytes 1572868
  56.1 18.8 %all-to-all-start.3 = ((bf16[4,256,256]{2,0,1:T(4,128)(2,1)}), bf16[4,256,256]{2,0,1:T(4,128)(2,1)S(1)}, u32[]{:S(2)}, u32[]{:S(2)}) async-start(bf16[4,256,256]{2,0,1:T(4,128)(2,1)} %copy.374), calls=%async_computation.3 | async-start | bytes 1048576 | tf_op jit(solution)/shard_map/all_to_all | solution.py:199
  74.8 12.0 %all-to-all-start = ((bf16[32,32,256]{2,0,1:T(8,128)(2,1)}), bf16[32,32,256]{2,0,1:T(8,128)(2,1)S(1)}, u32[]{:S(2)}, u32[]{:S(2)}) async-start(bf16[32,32,256]{2,0,1:T(8,128)(2,1)} %copy.364), calls=%async_computation | async-start | bytes 1048576 | tf_op jit(solution)/shard_map/all_to_all | solution.py:206
  86.9 11.8 %copy-start.2 = (bf16[32,32,256]{2,0,1:T(8,128)(2,1)}, bf16[32,32,256]{2,0,1:T(8,128)(2,1)S(1)}, u32[]{:S(2)}) copy-start(bf16[32,32,256]{2,0,1:T(8,128)(2,1)S(1)} %all-to-all-done) | copy-start | bytes 1572868
  86.9 10.4 %all-to-all-start.4 = ((bf16[32,32,256]{2,0,1:T(8,128)(2,1)}), bf16[32,32,256]{2,0,1:T(8,128)(2,1)S(1)}, u32[]{:S(2)}, u32[]{:S(2)}) async-start(bf16[32,32,256]{2,0,1:T(8,128)(2,1)} %copy.377), calls=%async_computation.4 | async-start | bytes 1048576 | tf_op jit(solution)/shard_map/all_to_all | solution.py:198
  90.7 8.9 %copy-start.40 = (f32[256]{0:T(256)S(1)}, f32[256]{0:T(256)}, u32[]{:S(2)}) copy-start(f32[256]{0:T(256)} %param.18) | copy-start | bytes 3076
  107.9 5.8 %copy-start.20 = (bf16[128,8,256]{0,2,1:T(8,128)(2,1)}, bf16[128,8,256]{0,2,1:T(8,128)(2,1)S(1)}, u32[]{:S(2)}) copy-start(bf16[128,8,256]{0,2,1:T(8,128)(2,1)S(1)} %copy.385) | copy-start | bytes 1572868
  151.7 6.1 %copy-start.3 = (bf16[32,32,256]{2,0,1:T(8,128)(2,1)S(1)}, bf16[32,32,256]{2,0,1:T(8,128)(2,1)}, u32[]{:S(2)}) copy-start(bf16[32,32,256]{2,0,1:T(8,128)(2,1)} %copy-done.2) | copy-start | bytes 1572868
  152.5 6.3 %copy-start.11 = (bf16[4,4,64,256]{3,2,1,0:T(8,128)(2,1)S(1)}, bf16[4,4,64,256]{3,2,1,0:T(8,128)(2,1)}, u32[]{:S(2)}) copy-start(bf16[4,4,64,256]{3,2,1,0:T(8,128)(2,1)} %copy-done.10) | copy-start | bytes 1572868
  153.6 10.8 %all-to-all-start.6 = ((bf16[128,8,256]{2,1,0:T(8,128)(2,1)}), bf16[128,8,256]{2,1,0:T(8,128)(2,1)}, u32[]{:S(2)}, u32[]{:S(2)}) async-start(bf16[128,8,256]{2,1,0:T(8,128)(2,1)} %copy.399), calls=%async_computation.6 | async-start | bytes 1048576 | tf_op jit(solution)/shard_map/all_to_all | solution.py:221
  159.3 10.9 %copy-start.6 = (bf16[128,8,256]{2,0,1:T(8,128)(2,1)S(1)}, bf16[128,8,256]{2,0,1:T(8,128)(2,1)}, u32[]{:S(2)}) copy-start(bf16[128,8,256]{2,0,1:T(8,128)(2,1)} %copy-done.4) | copy-start | bytes 1572868
  163.5 8.9 %copy-start.18 = (bf16[128,8,256]{2,0,1:T(8,128)(2,1)S(1)}, bf16[128,8,256]{2,0,1:T(8,128)(2,1)}, u32[]{:S(2)}) copy-start(bf16[128,8,256]{2,0,1:T(8,128)(2,1)} %copy-done.17) | copy-start | bytes 1572868
  166.3 18.8 %all-to-all-start.7 = ((bf16[32,32,256]{2,1,0:T(8,128)(2,1)}), bf16[32,32,256]{2,1,0:T(8,128)(2,1)S(1)}, u32[]{:S(2)}, u32[]{:S(2)}) async-start(bf16[32,32,256]{2,1,0:T(8,128)(2,1)} %bitcast.239), calls=%async_computation.7 | async-start | bytes 1048576 | tf_op jit(solution)/shard_map/all_to_all | solution.py:220
  169.8 144.5 %all-reduce.7.cloned.1.call-start = ((), (), s32[]{:S(2)}) async-start(), calls=%async_computation.9 | async-start | bytes 8388608 | tf_op jit(solution)/shard_map/psum | solution.py:233
  192.0 8.1 %copy-start.30 = (bf16[4,256,256]{1,2,0:T(8,128)(2,1)S(1)}, bf16[4,256,256]{1,2,0:T(8,128)(2,1)}, u32[]{:S(2)}) copy-start(bf16[4,256,256]{1,2,0:T(8,128)(2,1)} %copy-done.29) | copy-start | bytes 1572868
  208.1 5.4 %copy-start.19 = (bf16[32,8,4,256]{3,1,2,0:T(8,128)(2,1)S(1)}, bf16[32,8,4,256]{3,1,2,0:T(8,128)(2,1)}, u32[]{:S(2)}) copy-start(bf16[32,8,4,256]{3,1,2,0:T(8,128)(2,1)} %copy.437) | copy-start | bytes 1572868
  208.1 6.4 %copy-start.16 = (bf16[4,256,256]{2,1,0:T(8,128)(2,1)S(1)}, bf16[4,256,256]{2,1,0:T(8,128)(2,1)}, u32[]{:S(2)}) copy-start(bf16[4,256,256]{2,1,0:T(8,128)(2,1)} %copy-done.15) | copy-start | bytes 1572868
  217.3 97.0 %copy-start.31 = (bf16[4,256,256]{2,1,0:T(8,128)(2,1)S(1)}, bf16[4,256,256]{2,1,0:T(8,128)(2,1)}, u32[]{:S(2)}) copy-start(bf16[4,256,256]{2,1,0:T(8,128)(2,1)} %copy.406) | copy-start | bytes 1572868
  217.3 97.0 %copy-start.33 = (bf16[4,256,256]{2,1,0:T(8,128)(2,1)S(1)}, bf16[4,256,256]{2,1,0:T(8,128)(2,1)}, u32[]{:S(2)}) copy-start(bf16[4,256,256]{2,1,0:T(8,128)(2,1)} %copy.405) | copy-start | bytes 1572868
  217.3 97.0 %copy-start.37 = (bf16[256,768]{1,0:T(8,128)(2,1)S(1)}, bf16[256,768]{1,0:T(8,128)(2,1)}, u32[]{:S(2)}) copy-start(bf16[256,768]{1,0:T(8,128)(2,1)} %param.16) | copy-start | bytes 1179652
  217.3 207.4 %all-reduce.9.cloned.1.call-start = ((), (), s32[]{:S(2)}) async-start(), calls=%async_computation.10 | async-start | bytes 8388608 | tf_op jit(solution)/shard_map/psum | solution.py:232
  315.7 5.9 %copy-start.42 = (f32[256]{0:T(256)S(1)}, f32[256]{0:T(256)}, u32[]{:S(2)}) copy-start(f32[256]{0:T(256)} %get-tuple-element.73) | copy-start | bytes 3076
  315.7 5.9 %copy-start.43 = (f32[256]{0:T(256)S(1)}, f32[256]{0:T(256)}, u32[]{:S(2)}) copy-start(f32[256]{0:T(256)} %get-tuple-element.84) | copy-start | bytes 3076
  317.7 35.2 %all-to-all-start.8 = ((bf16[4,256,256]{2,0,1:T(4,128)(2,1)}), bf16[4,256,256]{2,0,1:T(4,128)(2,1)S(1)}, u32[]{:S(2)}, u32[]{:S(2)}) async-start(bf16[4,256,256]{2,0,1:T(4,128)(2,1)} %copy.409), calls=%async_computation.8 | async-start | bytes 1048576 | tf_op jit(solution)/shard_map/all_to_all | solution.py:230
  424.7 6.0 %copy-start.38 = (f32[256,256]{1,0:T(8,128)S(1)}, f32[256,256]{1,0:T(8,128)}, u32[]{:S(2)}) copy-start(f32[256,256]{1,0:T(8,128)} %get-tuple-element.152) | copy-start | bytes 786436
  424.7 6.7 %copy-start.24 = (f32[256,1024]{1,0:T(8,128)S(1)}, f32[256,1024]{1,0:T(8,128)}, u32[]{:S(2)}) copy-start(f32[256,1024]{1,0:T(8,128)} %get-tuple-element.154) | copy-start | bytes 3145732
  424.7 7.7 %copy-start.23 = (f32[1024,256]{1,0:T(8,128)S(1)}, f32[1024,256]{1,0:T(8,128)}, u32[]{:S(2)}) copy-start(f32[1024,256]{1,0:T(8,128)} %get-tuple-element.155) | copy-start | bytes 3145732
  426.9 6.4 %copy-start.1 = (bf16[256,1024]{1,0:T(8,128)(2,1)S(1)}, bf16[256,1024]{1,0:T(8,128)(2,1)}, u32[]{:S(2)}) copy-start(bf16[256,1024]{1,0:T(8,128)(2,1)} %param.22) | copy-start | bytes 1572868
  (24 other events, 67.0 us)
Sparse Core Ops, SparseCore 0:
  217.4 96.8 all-reduce.6
  318.5 106.0 all-reduce.8
